TPU v7x, 512 devices: a whole 4x8x8 slice. The times are simulated.
512 devices in a mesh: band: 32 (over z_hi, x, core), chan: 16 (over y, z_lo).
Axes of the slice: x: 4, y: 8, z: 8 (z_hi: 4, z_lo: 2; z = z_hi * 2 + z_lo), core: 2. Of those that a mesh axis runs over, the one named last changes fastest.
Arguments:
- image: bfloat16 [512, 128, 512], P('chan', 'band'), may hold values from -6 to 6
- filters: bfloat16 [9, 512, 512], P(None, None, 'chan'), may hold values from -0.09375 to 0.09375
- bias: bfloat16 [512], P('chan'), may hold values from -3 to 3
- upstream: bfloat16 [512, 128, 512], P('chan', 'band'), may hold values from -6 to 6
Outputs:
- features: bfloat16 [512, 128, 512], P('chan', 'band')
- image_grad: bfloat16 [512, 128, 512], P('chan', 'band')
All inputs are finite; a program needn't handle non-finite values.
Results may differ from a plain program's by a relative error of at most 0.001.
Values may be sent and summed in bfloat16 or wider, within the bound.
A program may use at most 64 MiB of HBM per device.

v0:
```python
import jax
import jax.numpy as jnp
from jax import lax
from jax.sharding import PartitionSpec as P


def with_halo(value, sides, width):
    for axis, dim in sides:
        size, length = (lax.axis_size(axis), value.shape[dim])
        up = [(i, (i + 1) % size) for i in range(size - 1)]
        down = [(j, i) for i, j in up]
        last = lax.slice_in_dim(value, length - width, length, axis=dim)
        first = lax.slice_in_dim(value, 0, width, axis=dim)
        before = lax.ppermute(last, axis, up)
        after = lax.ppermute(first, axis, down)
        value = jnp.concatenate([before, value, after], axis=dim)
    return value


def tap_forward(weights, source, row_count, col_count):
    result = None
    for tap_row in range(3):
        for tap_col in range(3):
            term = jnp.einsum(
                "oi,irc->orc",
                weights[tap_row * 3 + tap_col],
                source[:, tap_row : tap_row + row_count, tap_col : tap_col + col_count],
                preferred_element_type=jnp.float32,
            )
            result = term if result is None else result + term
    return result


def tap_backward(weights, source, row_count, col_count):
    result = None
    for tap_row in range(3):
        for tap_col in range(3):
            term = jnp.einsum(
                "oi,orc->irc",
                weights[tap_row * 3 + tap_col],
                source[
                    :, 2 - tap_row : 2 - tap_row + row_count, 2 - tap_col : 2 - tap_col + col_count
                ],
                preferred_element_type=jnp.float32,
            )
            result = term if result is None else result + term
    return result


def per_device(image, filters, bias, upstream):
    row_count = image.shape[1]
    col_count = image.shape[2]
    stacked = jnp.stack([image, upstream])
    with_rims = with_halo(stacked, (("band", 2),), 1)
    padded = jnp.pad(with_rims, ((0, 0), (0, 0), (0, 0), (1, 1)))
    outward = lax.all_to_all(filters, "chan", split_axis=1, concat_axis=2, tiled=True)
    w_part = outward
    forward_sum = tap_forward(
        w_part, lax.all_gather(padded[0], "chan", axis=0, tiled=True), row_count, col_count
    )
    w_part = filters
    grad_sum = tap_backward(
        w_part, lax.all_gather(padded[1], "chan", axis=0, tiled=True), row_count, col_count
    )
    features = (forward_sum + bias.astype(jnp.float32)[:, None, None]).astype(jnp.bfloat16)
    image_grad = grad_sum.astype(jnp.bfloat16)
    return (features, image_grad)


def solution(mesh):
    return jax.shard_map(
        per_device,
        mesh=mesh,
        in_specs=(
            P("chan", "band", None),
            P(None, None, "chan"),
            P("chan"),
            P("chan", "band", None),
        ),
        out_specs=(P("chan", "band", None), P("chan", "band", None)),
        check_vma=False,
    )
```

profile of v0, /device:TPU:18, one launch (start us, length us, event | category | flops | bytes accessed | tf_op | source)
XLA Modules:
  0.0 245.0 jit_solution(1787459723346832427)
XLA Ops:
  7.2 0.0 copy-start.3
  7.2 0.0 all-gather.7.cloned.1.call-start
  7.2 1.0 copy_bitcast_fusion.1
  8.3 1.9 collective-permute-start.1
  10.2 2.4 collective-permute-start
  12.6 0.0 collective-permute-done.1
  12.6 3.2 %collective-permute-done = bf16[2,32,1,512]{3,1,2,0:T(8,128)(2,1)S(1)} collective-permute-done((bf16[2,32,1,512]{3,1,2,0:T(8,128)(2,1)S(1)}, bf16[2,32,1,512]{3,1,2,0:T(8,128)(2,1)S(1)}, u32[]{:S(2)}, u32[]{:S(2)}) %collective-permute-start) | collective-permute-done | bytes 65568 | tf_op jit(solution)/shard_map/ppermute | solution.py:14
  15.8 0.3 select_maximum_fusion
  16.1 0.9 fusion.122
  16.9 0.0 all-gather.7.cloned.1.call-update
  17.0 0.0 all-gather.5.cloned.1.call-start
  17.0 0.7 all-gather.5.cloned.1.call-update
  17.7 0.0 copy-done.3
  17.7 0.0 copy-start.4
  17.7 2.0 copy.13
  19.7 2.0 reshape.52
  21.7 9.3 %all-to-all-start = ((bf16[16,2,4608]{2,1,0:T(2,128)(2,1)}), bf16[16,2,4608]{2,1,0:T(2,128)(2,1)S(1)}, u32[]{:S(2)}, u32[]{:S(2)}) async-start(bf16[16,2,4608]{2,1,0:T(2,128)(2,1)} %reshape.52), calls=%async_computation | async-start | bytes 589824 | tf_op jit(solution)/shard_map/all_to_all | solution.py:56
  30.9 0.0 copy-done.4
  31.0 10.4 %all-to-all-done = bf16[16,2,4608]{2,1,0:T(2,128)(2,1)S(1)} async-done(((bf16[16,2,4608]{2,1,0:T(2,128)(2,1)}), bf16[16,2,4608]{2,1,0:T(2,128)(2,1)S(1)}, u32[]{:S(2)}, u32[]{:S(2)}) %all-to-all-start) | async-done | bytes 294944 | tf_op jit(solution)/shard_map/all_to_all | solution.py:56
  41.4 1.4 reshape.53
  42.7 0.8 copy.20
  43.6 0.2 fusion.121
  43.8 0.2 reshape.33
  44.0 0.2 reshape.32
  44.1 0.2 reshape.31
  44.3 0.2 reshape.30
  44.4 0.2 reshape.29
  44.6 0.2 reshape.28
  44.8 0.2 reshape.27
  44.9 0.2 reshape.26
  45.1 0.2 reshape.25
  45.2 76.4 %all-gather.7.cloned.1.call-done = bf16[1,512,6,514]{3,1,2,0:T(8,128)(2,1)} async-done(((bf16[1,32,6,514]{3,1,2,0:T(8,128)(2,1)}), bf16[1,512,6,514]{3,1,2,0:T(8,128)(2,1)}) %all-gather.7.cloned.1.call-update) | async-done | bytes 3158032 | tf_op jit(solution)/shard_map/all_gather | solution.py:63
  121.6 0.0 copy-start
  121.6 2.2 fusion
  123.8 2.5 %fusion.2 = f32[4,512,32]{1,2,0:T(8,128)S(1)} fusion(bf16[512,6,514]{2,0,1:T(8,128)(2,1)} %bitcast.80, bf16[9,512,32]{1,2,0:T(8,128)(2,1)S(1)} %copy-done.3), kind=kOutput, calls=%fused_computation.2 | convolution fusion | flops 67108864 | bytes 2392064 | tf_op jit(solution)/shard_map/oi,orc->irc/dot_general | solution.py:38
  126.3 0.0 copy-done
  126.4 0.8 fusion.4
  127.1 0.5 fusion.6
  127.6 0.8 fusion.8
  128.4 0.8 fusion.10
  129.2 0.5 fusion.12
  129.6 0.8 fusion.14
  130.4 94.7 %all-gather.5.cloned.1.call-done = bf16[1,512,6,514]{3,1,2,0:T(8,128)(2,1)} async-done(((bf16[1,32,6,514]{3,1,2,0:T(8,128)(2,1)}), bf16[1,512,6,514]{3,1,2,0:T(8,128)(2,1)}) %all-gather.5.cloned.1.call-update) | async-done | bytes 3158032 | tf_op jit(solution)/shard_map/all_gather | solution.py:59
  225.1 0.0 copy-start.2
  225.1 2.7 %fusion.18 = f32[4,512,32]{1,2,0:T(8,128)S(1)} fusion(bf16[32,512,1]{1,0,2:T(8,128)(2,1)S(1)} %reshape.33, bf16[512,6,514]{2,0,1:T(8,128)(2,1)} %bitcast.88), kind=kOutput, calls=%fused_computation.18 | convolution fusion | flops 67108864 | bytes 2392064 | tf_op jit(solution)/shard_map/oi,irc->orc/dot_general | solution.py:24
  227.8 2.5 %fusion.20 = f32[4,512,32]{1,2,0:T(8,128)S(1)} fusion(bf16[32,512,1]{1,0,2:T(8,128)(2,1)S(1)} %reshape.32, bf16[512,6,514]{2,0,1:T(8,128)(2,1)} %bitcast.89), kind=kOutput, calls=%fused_computation.20 | convolution fusion | flops 67108864 | bytes 2392064 | tf_op jit(solution)/shard_map/oi,irc->orc/dot_general | solution.py:24
  230.3 0.0 copy-done.2
  230.3 0.5 fusion.22
  230.8 0.8 fusion.24
  231.6 0.8 fusion.26
  232.4 0.5 fusion.28
  232.8 0.8 fusion.30
  233.6 0.8 fusion.32
  234.4 0.0 copy-start.1
  234.4 0.5 fusion.93
  235.0 0.8 copy.15
  235.7 0.9 copy-done.1
  236.6 0.8 fusion.96
  237.4 0.8 copy.16
  (2 shorter events, 0.0 us)
Async XLA Ops:
  7.2 10.6 %copy-start.3 = (bf16[9,512,32]{1,2,0:T(8,128)(2,1)S(1)}, bf16[9,512,32]{1,2,0:T(8,128)(2,1)}, u32[]{:S(2)}) copy-start(bf16[9,512,32]{1,2,0:T(8,128)(2,1)} %param.5) | copy-start | bytes 884740
  7.2 114.4 %all-gather.7.cloned.1.call-start = ((), (), s32[]{:S(2)}) async-start(), calls=%async_computation.2 | async-start | bytes 4177920 | tf_op jit(solution)/shard_map/all_gather | solution.py:63
  8.3 4.3 %collective-permute-start.1 = (bf16[2,32,1,512]{3,1,2,0:T(8,128)(2,1)S(1)}, bf16[2,32,1,512]{3,1,2,0:T(8,128)(2,1)S(1)}, u32[]{:S(2)}, u32[]{:S(2)}) collective-permute-start(bf16[2,32,1,512]{3,1,2,0:T(8,128)(2,1)S(1)} %get-tuple-element.18), channel_id=1, source_target_pairs={{16,0},{32,16},{48,32},{64,48},{80,64},{96,80},{112,96},{128,112},... | collective-permute-start | bytes 196616 | tf_op jit(solution)/shard_map/ppermute | solution.py:15
  10.2 5.6 %collective-permute-start = (bf16[2,32,1,512]{3,1,2,0:T(8,128)(2,1)S(1)}, bf16[2,32,1,512]{3,1,2,0:T(8,128)(2,1)S(1)}, u32[]{:S(2)}, u32[]{:S(2)}) collective-permute-start(bf16[2,32,1,512]{3,1,2,0:T(8,128)(2,1)S(1)} %get-tuple-element.17), channel_id=1, source_target_pairs={{0,16},{16,32},{32,48},{48,64},{64,80},{80,96},{96,112},{112,128},... | collective-permute-start | bytes 196616 | tf_op jit(solution)/shard_map/ppermute | solution.py:14
  17.0 208.1 %all-gather.5.cloned.1.call-start = ((), (), s32[]{:S(2)}) async-start(), calls=%async_computation.1 | async-start | bytes 4177920 | tf_op jit(solution)/shard_map/all_gather | solution.py:59
  17.7 13.2 %copy-start.4 = (bf16[32]{0:T(256)(128)(2,1)S(1)}, bf16[32]{0:T(256)(128)(2,1)}, u32[]{:S(2)}) copy-start(bf16[32]{0:T(256)(128)(2,1)} %param.6) | copy-start | bytes 196
  21.7 19.7 %all-to-all-start = ((bf16[16,2,4608]{2,1,0:T(2,128)(2,1)}), bf16[16,2,4608]{2,1,0:T(2,128)(2,1)S(1)}, u32[]{:S(2)}, u32[]{:S(2)}) async-start(bf16[16,2,4608]{2,1,0:T(2,128)(2,1)} %reshape.52), calls=%async_computation | async-start | bytes 589824 | tf_op jit(solution)/shard_map/all_to_all | solution.py:56
  121.6 4.7 %copy-start = (bf16[1,512,6,514]{3,1,2,0:T(8,128)(2,1)S(1)}, bf16[1,512,6,514]{3,1,2,0:T(8,128)(2,1)}, u32[]{:S(2)}) copy-start(bf16[1,512,6,514]{3,1,2,0:T(8,128)(2,1)} %all-gather.7.cloned.1.call-done) | copy-start | bytes 9474052
  225.1 5.2 %copy-start.2 = (bf16[1,512,6,514]{3,1,2,0:T(8,128)(2,1)S(1)}, bf16[1,512,6,514]{3,1,2,0:T(8,128)(2,1)}, u32[]{:S(2)}) copy-start(bf16[1,512,6,514]{3,1,2,0:T(8,128)(2,1)} %all-gather.5.cloned.1.call-done) | copy-start | bytes 9474052
  234.4 2.2 copy-start.1
Sparse Core Ops, SparseCore 0:
  17.1 104.4 all-gather.6
  123.7 101.3 all-gather.4
where the time goes:
time: 245 us
  waiting for transfers between devices  185 us (76%)
  matrix products  19.4 us (8%)
  between operations  14.2 us (6%)
  starting transfers between devices  13.7 us (6%)
  local copies, waits for them, and re-layouts  12.1 us (5%)
    all_gather x1, waiting for transfers between devices, per_device(): lax.all_gather(padded[0], 'chan', axis=0, tiled=True)  94.7 us
    all_gather x1, waiting for transfers between devices, per_device(): lax.all_gather(padded[1], 'chan', axis=0, tiled=True)  76.4 us
    all_to_all x1, waiting for transfers between devices, per_device(): lax.all_to_all(filters, 'chan', split_axis=1, concat_axis=2, tiled=True)  10.4 us
    dot_general x9, matrix products, tap_forward(): jnp.einsum('oi,irc->orc', weights[tap_row * 3 + tap_col], source[:, tap_r...  9.83 us
    dot_general x9, matrix products, tap_backward(): jnp.einsum('oi,orc->irc', weights[tap_row * 3 + tap_col], source[:, 2 - t...  9.61 us
    all_to_all x1, starting transfers between devices, per_device(): lax.all_to_all(filters, 'chan', split_axis=1, concat_axis=2, tiled=True)  9.26 us
    unnamed x15, local copies, waits for them, and re-layouts  7.71 us
  transfers between devices with their start and end apart: 5, of which 4 were waited for; matrix products, arithmetic and copies ran while one was open for 7% of the time, Pallas kernels for 0%

commit v1 on v0

--- a/solution.py
+++ b/solution.py
@@ -56,7 +56,12 @@
     outward = lax.all_to_all(filters, "chan", split_axis=1, concat_axis=2, tiled=True)
     w_part = outward
     forward_sum = tap_forward(
-        w_part, lax.all_gather(padded[0], "chan", axis=0, tiled=True), row_count, col_count
+        w_part,
+        jnp.concatenate(
+            lax.all_to_all(jnp.stack([padded[0]] * lax.axis_size("chan")), "chan", 0, 0), axis=0
+        ),
+        row_count,
+        col_count,
     )
     w_part = filters
     grad_sum = tap_backward(

time: 245 us -> 223 us (0.910)
  the two profiles are of different devices: /device:TPU:18 before, /device:TPU:90 now
where the time goes in v1:
time: 223 us
  waiting for transfers between devices  145 us (65%)
  blocking collectives  18.7 us (8%)
  local copies, waits for them, and re-layouts  16.3 us (7%)
  matrix products  15.9 us (7%)
  between operations  14.2 us (6%)
  starting transfers between devices  12.9 us (6%)
    all_gather x1, waiting for transfers between devices, per_device(): lax.all_gather(padded[1], 'chan', axis=0, tiled=True)  143 us
    all_to_all x1, blocking collectives, per_device(): lax.all_to_all(filters, 'chan', split_axis=1, concat_axis=2, tiled=True)  18.7 us
    dot_general x9, matrix products, tap_backward(): jnp.einsum('oi,orc->irc', weights[tap_row * 3 + tap_col], source[:, 2 - t...  9.69 us
    all_to_all x1, starting transfers between devices, per_device(): lax.all_to_all(jnp.stack([padded[0]] * lax.axis_size('chan')), 'chan', 0, 0)  7.26 us
    unnamed x11, local copies, waits for them, and re-layouts  7.03 us
    dot_general x9, matrix products, tap_forward(): jnp.einsum('oi,irc->orc', weights[tap_row * 3 + tap_col], source[:, tap_r...  6.25 us
  transfers between devices with their start and end apart: 4, of which 2 were waited for; matrix products, arithmetic and copies ran while one was open for 9% of the time, Pallas kernels for 0%

profile of v1, /device:TPU:90, one launch (start us, length us, event | category | flops | bytes accessed | tf_op | source)
XLA Modules:
  0.0 222.8 jit_solution(8628876053817600223)
XLA Ops:
  7.2 0.0 all-gather.3.cloned.1.call-start
  7.2 1.0 copy_bitcast_fusion.1
  8.2 1.9 collective-permute-start
  10.2 3.6 %collective-permute-start.1 = (bf16[2,32,1,512]{3,1,2,0:T(8,128)(2,1)S(1)}, bf16[2,32,1,512]{3,1,2,0:T(8,128)(2,1)S(1)}, u32[]{:S(2)}, u32[]{:S(2)}) collective-permute-start(bf16[2,32,1,512]{3,1,2,0:T(8,128)(2,1)S(1)} %get-tuple-element.18), channel_id=1, source_target_pairs={{16,0},{32,16},{48,32},{64,48},{80,64},{96,80},{112,96},{128,112},... | collective-permute-start | bytes 196616 | tf_op jit(solution)/shard_map/ppermute | solution.py:15
  13.8 0.0 collective-permute-done
  13.8 1.9 collective-permute-done.1
  15.7 0.3 select_maximum_fusion
  16.0 0.7 fusion.122
  16.7 0.0 all-gather.3.cloned.1.call-update
  16.7 2.9 %copy.14 = bf16[9,512,32]{2,0,1:T(8,128)(2,1)S(1)} copy(bf16[9,512,32]{1,2,0:T(8,128)(2,1)} %param.5) | data formatting | bytes 589824 | tf_op args[1]
  19.6 1.3 reshape.56
  20.9 18.7 %all_to_all.20 = bf16[16,2,4608]{2,1,0:T(2,128)(2,1)S(1)} all-to-all(bf16[16,2,4608]{2,1,0:T(2,128)(2,1)S(1)} %reshape.56), channel_id=1, replica_groups=mesh['band'=32,'chan'=16] {'chan'}, dimensions={0} | all-to-all | bytes 589824 | tf_op jit(solution)/shard_map/all_to_all | solution.py:56
  39.5 2.4 %stack.15 = bf16[16,32,6,514]{3,1,2,0:T(8,128)(2,1)} broadcast(bf16[32,6,514]{2,0,1:T(8,128)(2,1)S(1)} %get-tuple-element.16), dimensions={1,2,3} | broadcast | bytes 3355392 | tf_op jit(solution)/shard_map/stack | solution.py:61
  42.0 0.0 copy-start.2
  42.0 7.3 %all-to-all-start = ((bf16[16,32,6,514]{3,1,2,0:T(8,128)(2,1)}), bf16[16,32,6,514]{3,1,2,0:T(8,128)(2,1)}, u32[]{:S(2)}, u32[]{:S(2)}) async-start(bf16[16,32,6,514]{3,1,2,0:T(8,128)(2,1)} %stack.15), calls=%async_computation | async-start | bytes 7864320 | tf_op jit(solution)/shard_map/all_to_all | solution.py:61
  49.2 0.0 copy-done.2
  49.2 1.4 reshape.57
  50.6 0.0 copy-start.1
  50.6 0.8 copy.21
  51.5 0.2 fusion.121
  51.7 0.2 reshape.32
  51.9 0.2 reshape.31
  52.0 0.2 reshape.30
  52.2 0.2 reshape.33
  52.4 0.2 reshape.34
  52.5 0.2 reshape.35
  52.7 0.2 reshape.36
  52.8 0.2 reshape.37
  53.0 0.2 reshape.29
  53.1 142.7 %all-gather.3.cloned.1.call-done = bf16[1,512,6,514]{3,1,2,0:T(8,128)(2,1)} async-done(((bf16[1,32,6,514]{3,1,2,0:T(8,128)(2,1)}), bf16[1,512,6,514]{3,1,2,0:T(8,128)(2,1)}) %all-gather.3.cloned.1.call-update) | async-done | bytes 3158032 | tf_op jit(solution)/shard_map/all_gather | solution.py:68
  195.9 0.0 copy-start
  195.9 0.0 copy-done.1
  195.9 2.2 fusion
  198.1 2.5 %fusion.10 = f32[4,512,32]{1,2,0:T(8,128)S(1)} fusion(bf16[512,6,514]{2,0,1:T(8,128)(2,1)} %bitcast.91, bf16[9,512,32]{1,2,0:T(8,128)(2,1)S(1)} %copy-done.1), kind=kOutput, calls=%fused_computation.10 | convolution fusion | flops 67108864 | bytes 2392064 | tf_op jit(solution)/shard_map/oi,orc->irc/dot_general | solution.py:38
  200.6 0.0 copy-done
  200.6 0.5 fusion.12
  201.1 0.8 fusion.14
  201.9 0.8 fusion.2
  202.7 0.8 fusion.4
  203.5 0.5 fusion.6
  203.9 0.8 fusion.8
  204.7 0.8 fusion.96
  205.6 0.8 copy.17
  206.3 0.0 all-to-all-done
  206.3 2.6 %copy.13 = bf16[16,32,6,514]{3,1,0,2:T(8,128)(2,1)S(1)} copy(bf16[16,32,6,514]{3,1,2,0:T(8,128)(2,1)} %all-to-all-done) | data formatting | bytes 6316032 | tf_op jit(solution)/shard_map/all_to_all | solution.py:61
  208.9 0.5 fusion.28
  209.4 0.8 fusion.30
  210.2 0.8 fusion.32
  211.0 0.8 fusion.26
  211.8 0.8 fusion.24
  212.6 0.5 fusion.22
  213.0 0.8 fusion.20
  213.8 0.8 fusion.18
  214.6 0.5 fusion.93
  215.2 0.8 copy.16
  (2 shorter events, 0.0 us)
Async XLA Ops:
  7.2 188.7 %all-gather.3.cloned.1.call-start = ((), (), s32[]{:S(2)}) async-start(), calls=%async_computation.2 | async-start | bytes 4177920 | tf_op jit(solution)/shard_map/all_gather | solution.py:68
  8.2 5.6 %collective-permute-start = (bf16[2,32,1,512]{3,1,2,0:T(8,128)(2,1)S(1)}, bf16[2,32,1,512]{3,1,2,0:T(8,128)(2,1)S(1)}, u32[]{:S(2)}, u32[]{:S(2)}) collective-permute-start(bf16[2,32,1,512]{3,1,2,0:T(8,128)(2,1)S(1)} %get-tuple-element.17), channel_id=1, source_target_pairs={{0,16},{16,32},{32,48},{48,64},{64,80},{80,96},{96,112},{112,128},... | collective-permute-start | bytes 196616 | tf_op jit(solution)/shard_map/ppermute | solution.py:14
  10.2 5.5 %collective-permute-start.1 = (bf16[2,32,1,512]{3,1,2,0:T(8,128)(2,1)S(1)}, bf16[2,32,1,512]{3,1,2,0:T(8,128)(2,1)S(1)}, u32[]{:S(2)}, u32[]{:S(2)}) collective-permute-start(bf16[2,32,1,512]{3,1,2,0:T(8,128)(2,1)S(1)} %get-tuple-element.18), channel_id=1, source_target_pairs={{16,0},{32,16},{48,32},{64,48},{80,64},{96,80},{112,96},{128,112},... | collective-permute-start | bytes 196616 | tf_op jit(solution)/shard_map/ppermute | solution.py:15
  42.0 7.3 %copy-start.2 = (bf16[32]{0:T(256)(128)(2,1)S(1)}, bf16[32]{0:T(256)(128)(2,1)}, u32[]{:S(2)}) copy-start(bf16[32]{0:T(256)(128)(2,1)} %param.6) | copy-start | bytes 196
  42.0 164.4 %all-to-all-start = ((bf16[16,32,6,514]{3,1,2,0:T(8,128)(2,1)}), bf16[16,32,6,514]{3,1,2,0:T(8,128)(2,1)}, u32[]{:S(2)}, u32[]{:S(2)}) async-start(bf16[16,32,6,514]{3,1,2,0:T(8,128)(2,1)} %stack.15), calls=%async_computation | async-start | bytes 7864320 | tf_op jit(solution)/shard_map/all_to_all | solution.py:61
  50.6 145.2 %copy-start.1 = (bf16[9,512,32]{1,2,0:T(8,128)(2,1)S(1)}, bf16[9,512,32]{1,2,0:T(8,128)(2,1)}, u32[]{:S(2)}) copy-start(bf16[9,512,32]{1,2,0:T(8,128)(2,1)} %param.5) | copy-start | bytes 884740
  195.9 4.7 %copy-start = (bf16[1,512,6,514]{3,1,2,0:T(8,128)(2,1)S(1)}, bf16[1,512,6,514]{3,1,2,0:T(8,128)(2,1)}, u32[]{:S(2)}) copy-start(bf16[1,512,6,514]{3,1,2,0:T(8,128)(2,1)} %all-gather.3.cloned.1.call-done) | copy-start | bytes 9474052
Sparse Core Ops, SparseCore 0:
  16.9 178.9 all-gather.2
